TPU v7x, 32 devices: a whole 2x2x4 slice. The times are simulated.
32 devices in a mesh: dp: 4 (over y, x), ctx: 8 (over z, core).
Axes of the slice: x: 2, y: 2, z: 4, core: 2. Of those that a mesh axis runs over, the one named last changes fastest.
Arguments:
- tokens: bfloat16 [4, 1024, 2048], P('dp', 'ctx'), may hold values from -6 to 6
- positions: int32 [4, 1024], P('dp', 'ctx'), may hold values from 0 to 1023, as said below
- norm_gain: float32 [2048], replicated, may hold values from 0.5 to 1.5
- norm_bias: float32 [2048], replicated, may hold values from -1.8 to 1.8
- qkv_weight: bfloat16 [2048, 6144], P('ctx'), may hold values from -0.125 to 0.125
- qkv_bias: float32 [6144], replicated, may hold values from -1.8 to 1.8
- dense_weight: bfloat16 [2048, 2048], P('ctx'), may hold values from -2 to 2
- dense_bias: float32 [2048], replicated, may hold values from -1.8 to 1.8
- up_weight: bfloat16 [2048, 8192], P('ctx'), may hold values from -0.125 to 0.125
- up_bias: float32 [8192], replicated, may hold values from -1.8 to 1.8
- down_weight: bfloat16 [8192, 2048], P('ctx'), may hold values from -0.0625 to 0.0625
- down_bias: float32 [2048], replicated, may hold values from -1.8 to 1.8
- clip_limit: int32 [32], replicated, may hold values from 3 to 11
- cotangent: bfloat16 [4, 1024, 2048], P('dp', 'ctx'), may hold values from -6 to 6
Outputs:
- layer_out: bfloat16 [4, 1024, 2048], P('dp', 'ctx')
- tokens_grad: float32 [4, 1024, 2048], P('dp', 'ctx')
- norm_gain_grad: float32 [2048], replicated
- norm_bias_grad: float32 [2048], replicated
- qkv_weight_grad: float32 [2048, 6144], P('ctx')
- qkv_bias_grad: float32 [6144], replicated
- dense_weight_grad: float32 [2048, 2048], P('ctx')
- dense_bias_grad: float32 [2048], replicated
- up_weight_grad: float32 [2048, 8192], P('ctx')
- up_bias_grad: float32 [8192], replicated
- down_weight_grad: float32 [8192, 2048], P('ctx')
- down_bias_grad: float32 [2048], replicated
- head_maxima: float32 [32], replicated
- clipped_weight: float32 [2048, 4096], P('ctx')
- clipped_bias: float32 [4096], replicated
Inputs may be any that keep to these rules, and one draw needn't show every extreme that they name: `positions`: within each sequence the ids rise by one from 0 at its first token and return to 0 at the first token of each packed document; the first sequence holds a single document.
All inputs are finite; a program needn't handle non-finite values.
Results may differ from a plain program's by a relative error of at most 0.017.
Values may be sent and summed in bfloat16 or wider, within the bound.
No kernel may reach another device: no remote copies, remote signals or barrier semaphores. Data moves between devices by JAX's collectives and lax.ppermute only.
A program may use at most 512 MiB of HBM per device.

v0:
```python
from functools import partial
import jax
import jax.numpy as jnp
from jax import lax
from jax.sharding import PartitionSpec as P

ROT = 32
epsilon = 1e-05
masked_score = -1e30
rope_base = 10000.0
no_batch = ((), ())


def from_behind(value, axis, steps):
    count = lax.axis_size(axis)
    leading, last = (max(0, -steps), min(count, count - steps))
    return lax.ppermute(value, axis, [(source, source + steps) for source in range(leading, last)])


def from_behind_2(value, axis, steps):
    count = lax.axis_size(axis)
    pairs = [(source, (source + steps) % count) for source in range(count)]
    return lax.ppermute(value, axis, pairs)


def rotary_tables(positions):
    half_rot = ROT // 2
    frequency = rope_base ** (-(jnp.arange(half_rot, dtype=jnp.float32) * 2.0 / ROT))
    angles = positions.astype(jnp.float32)[..., None] * frequency
    cosine = jnp.cos(angles)
    sine_part = jnp.sin(angles)
    return (
        jnp.concatenate([cosine, cosine], -1)[..., None, :],
        jnp.concatenate([sine_part, sine_part], -1)[..., None, :],
    )


def rotate(values, cosine, sine_part):
    half_rot = ROT // 2
    turned = values[..., :ROT]
    swapped = jnp.concatenate([-turned[..., half_rot:], turned[..., :half_rot]], -1)
    return jnp.concatenate([turned * cosine + swapped * sine_part, values[..., ROT:]], -1)


def rotate_back(gradient, cosine, sine_part):
    half_rot = ROT // 2
    turned = gradient[..., :ROT]
    scaled = turned * sine_part
    swapped = jnp.concatenate([scaled[..., half_rot:], -scaled[..., :half_rot]], -1)
    return jnp.concatenate([turned * cosine + swapped, gradient[..., ROT:]], -1)


def contract_last(left, right):
    return lax.dot_general(
        left, right, (((1,), (1,)), no_batch), preferred_element_type=jnp.float32
    )


def contract_first(left, right):
    return lax.dot_general(
        left, right, (((0,), (0,)), no_batch), preferred_element_type=jnp.float32
    )


def attend_block(cycle_state, queries, piece_keys, piece_values, allowed, score_scale):
    accumulated, run_max, run_sum = cycle_state
    scores = (
        jnp.einsum("sqhd,skhd->shqk", queries, piece_keys, preferred_element_type=jnp.float32)
        * score_scale
    )
    scores = jnp.where(allowed, scores, masked_score)
    new_max = jnp.maximum(run_max, jnp.max(scores, axis=-1))
    prob_block = jnp.where(allowed, jnp.exp(scores - new_max[..., None]), 0.0)
    shrink = jnp.exp(run_max - new_max)
    run_sum = run_sum * shrink + jnp.sum(prob_block, axis=-1)
    accumulated = accumulated * shrink[..., None] + jnp.einsum(
        "shqk,skhd->shqd",
        prob_block.astype(jnp.bfloat16),
        piece_values,
        preferred_element_type=jnp.float32,
    )
    return (accumulated, new_max, run_sum)


def per_device(
    tokens,
    positions,
    norm_gain,
    norm_bias,
    qkv_weight,
    qkv_bias,
    dense_weight,
    dense_bias,
    up_weight,
    up_bias,
    down_weight,
    down_bias,
    clip_limit,
    cotangent,
):
    seq_count, stretch_len, model_width = tokens.shape
    head_count = clip_limit.shape[0]
    head_dim = model_width // head_count
    row_count = seq_count * stretch_len
    ctx_size = lax.axis_size("ctx")
    ctx_index = lax.axis_index("ctx")
    score_scale = head_dim ** (-0.5)
    own_rows = qkv_weight.shape[0]
    ff_rows = down_weight.shape[0]
    ff_width = up_weight.shape[1]
    qkv_width = 3 * model_width
    inputs = tokens.reshape(row_count, model_width).astype(jnp.float32)
    centre = inputs - jnp.mean(inputs, axis=-1, keepdims=True)
    inv_std = lax.rsqrt(jnp.mean(centre * centre, axis=-1, keepdims=True) + epsilon)
    normed = centre * inv_std
    hidden = (normed * norm_gain + norm_bias).astype(jnp.bfloat16)
    in_local = jnp.concatenate([qkv_weight, up_weight], axis=1)
    out_local = jnp.concatenate([dense_weight, down_weight], axis=0)
    columns = hidden
    projected = jnp.dot(
        columns,
        lax.all_gather(in_local, "ctx", axis=0, tiled=True),
        preferred_element_type=jnp.float32,
    )
    joined = projected[:, :qkv_width] + qkv_bias
    upward = projected[:, qkv_width:] + up_bias
    cosine, sine_part = rotary_tables(positions)
    shaped = joined.reshape(seq_count, stretch_len, 3, head_count, head_dim)
    queries = rotate(shaped[:, :, 0], cosine, sine_part).astype(jnp.bfloat16)
    keys = rotate(shaped[:, :, 1], cosine, sine_part).astype(jnp.bfloat16)
    values = shaped[:, :, 2].astype(jnp.bfloat16)
    key_pack = keys.reshape(seq_count, stretch_len, model_width)
    value_pack = values.reshape(seq_count, stretch_len, model_width)
    query_time = ctx_index * stretch_len + jnp.arange(stretch_len, dtype=jnp.int32)
    start_state = (
        jnp.zeros((seq_count, head_count, stretch_len, head_dim), jnp.float32),
        jnp.full((seq_count, head_count, stretch_len), masked_score, jnp.float32),
        jnp.zeros((seq_count, head_count, stretch_len), jnp.float32),
    )
    cycle_state = start_state
    pieces = (
        lax.all_gather(key_pack, "ctx", axis=1, tiled=True),
        lax.all_gather(value_pack, "ctx", axis=1, tiled=True),
    )
    block_count = pieces[0].shape[1] // stretch_len
    key_blocks = pieces[0].reshape(seq_count, block_count, stretch_len, head_count, head_dim)
    value_blocks = pieces[1].reshape(seq_count, block_count, stretch_len, head_count, head_dim)

    def inner_step(carried, block_index):
        piece_keys = lax.dynamic_index_in_dim(key_blocks, block_index, 1, keepdims=False)
        piece_values = lax.dynamic_index_in_dim(value_blocks, block_index, 1, keepdims=False)
        key_time = block_index * stretch_len + jnp.arange(stretch_len, dtype=jnp.int32)
        allowed = query_time[:, None] >= key_time[None, :]
        return (
            attend_block(carried, queries, piece_keys, piece_values, allowed, score_scale),
            None,
        )

    cycle_state, unused_out = lax.scan(
        inner_step, cycle_state, jnp.arange(block_count, dtype=jnp.int32)
    )
    accumulated, row_max, row_sum = cycle_state
    head_maxima = lax.pmax(jnp.max(row_max, axis=(0, 2)), ("dp", "ctx"))
    mixed_rows = jnp.transpose(accumulated / row_sum[..., None], (0, 2, 1, 3))
    log_sum = row_max + jnp.log(row_sum)
    attended = mixed_rows.reshape(row_count, model_width).astype(jnp.bfloat16)
    activated = jax.nn.gelu(upward, approximate=True).astype(jnp.bfloat16)
    left_stack = jnp.concatenate(
        [
            attended.reshape(row_count, ctx_size, own_rows),
            activated.reshape(row_count, ctx_size, ff_rows),
        ],
        axis=2,
    ).reshape(row_count, -1)
    columns = left_stack
    branch_sum = jnp.dot(
        columns,
        lax.all_gather(out_local, "ctx", axis=0, tiled=True),
        preferred_element_type=jnp.float32,
    )
    layer_out = (inputs + branch_sum + dense_bias + down_bias).astype(jnp.bfloat16)
    grad_out = cotangent.reshape(row_count, model_width)
    left_grad = contract_last(grad_out, lax.all_gather(out_local, "ctx", axis=0, tiled=True))
    split_grad = left_grad.reshape(row_count, ctx_size, own_rows + ff_rows)
    mixed_grad = split_grad[:, :, :own_rows].reshape(row_count, model_width)
    act_grad = split_grad[:, :, own_rows:].reshape(row_count, ff_width)
    stack_owned, hidden_owned = (
        lax.all_to_all(left_stack, "ctx", split_axis=1, concat_axis=0, tiled=True),
        lax.all_to_all(hidden, "ctx", split_axis=1, concat_axis=0, tiled=True),
    )
    columns = stack_owned
    out_grad_local = contract_first(columns, lax.all_gather(grad_out, "ctx", axis=0, tiled=True))
    out_bias_grad = jnp.sum(grad_out.astype(jnp.float32), axis=0)
    unused_value, gelu_back = jax.vjp(partial(jax.nn.gelu, approximate=True), upward)
    up_grad_rows = gelu_back(act_grad)[0].astype(jnp.bfloat16)
    mixed_grad_low = mixed_grad.astype(jnp.bfloat16).reshape(
        seq_count, stretch_len, head_count, head_dim
    )
    row_delta = jnp.transpose(
        jnp.sum(mixed_grad_low.astype(jnp.float32) * mixed_rows, axis=-1), (0, 2, 1)
    )

    def back_block(cycle_state, offset):
        kv_stack, kv_grad, query_grad = cycle_state
        source = (ctx_index - offset) % ctx_size
        key_time = source * stretch_len + jnp.arange(stretch_len, dtype=jnp.int32)
        allowed = query_time[:, None] >= key_time[None, :]
        piece_keys = kv_stack[0].reshape(seq_count, stretch_len, head_count, head_dim)
        piece_values = kv_stack[1].reshape(seq_count, stretch_len, head_count, head_dim)
        scores = (
            jnp.einsum("sqhd,skhd->shqk", queries, piece_keys, preferred_element_type=jnp.float32)
            * score_scale
        )
        scores = jnp.where(allowed, scores, masked_score)
        prob_block = jnp.where(allowed, jnp.exp(scores - log_sum[..., None]), 0.0)
        value_step = jnp.einsum(
            "shqk,sqhd->skhd",
            prob_block.astype(jnp.bfloat16),
            mixed_grad_low,
            preferred_element_type=jnp.float32,
        )
        prob_grad = jnp.einsum(
            "sqhd,skhd->shqk", mixed_grad_low, piece_values, preferred_element_type=jnp.float32
        )
        score_grad = (prob_block * (prob_grad - row_delta[..., None])).astype(jnp.bfloat16)
        query_grad = (
            query_grad
            + jnp.einsum(
                "shqk,skhd->sqhd", score_grad, piece_keys, preferred_element_type=jnp.float32
            )
            * score_scale
        )
        key_step = (
            jnp.einsum("shqk,sqhd->skhd", score_grad, queries, preferred_element_type=jnp.float32)
            * score_scale
        )
        kv_grad = kv_grad + jnp.stack(
            [
                key_step.reshape(seq_count, stretch_len, model_width),
                value_step.reshape(seq_count, stretch_len, model_width),
            ]
        )
        return (kv_stack, kv_grad, query_grad)

    def move_keys(cycle_state):
        shifted = from_behind(cycle_state[0], "ctx", 1)
        return (shifted, cycle_state[1], cycle_state[2])

    def move_grads(cycle_state):
        shifted = from_behind_2(cycle_state[1].astype(jnp.bfloat16), "ctx", 1).astype(jnp.float32)
        return (cycle_state[0], shifted, cycle_state[2])

    def cycle_turn(offset, cycle_state):
        return move_grads(move_keys(back_block(cycle_state, offset)))

    cycle_state = (
        jnp.stack([key_pack, value_pack]),
        jnp.zeros((2, seq_count, stretch_len, model_width), jnp.float32),
        jnp.zeros((seq_count, stretch_len, head_count, head_dim), jnp.float32),
    )
    cycle_state = lax.fori_loop(0, ctx_size - 1, cycle_turn, cycle_state)
    cycle_state = move_grads(back_block(cycle_state, ctx_size - 1))
    kv_grad = cycle_state[1]
    query_pre = rotate_back(cycle_state[2], cosine, sine_part)
    key_pre = rotate_back(
        kv_grad[0].reshape(seq_count, stretch_len, head_count, head_dim), cosine, sine_part
    )
    value_pre = kv_grad[1].reshape(seq_count, stretch_len, head_count, head_dim)
    joined_low = (
        jnp.stack([query_pre, key_pre, value_pre], axis=2)
        .reshape(row_count, qkv_width)
        .astype(jnp.bfloat16)
    )
    qkv_bias_local = jnp.sum(joined_low.astype(jnp.float32), axis=0)
    up_bias_local = jnp.sum(up_grad_rows.astype(jnp.float32), axis=0)
    both_grads = jnp.concatenate([joined_low, up_grad_rows], axis=1)
    hidden_grad = contract_last(both_grads, lax.all_gather(in_local, "ctx", axis=0, tiled=True))
    columns = hidden_owned
    in_grad_local = contract_first(columns, lax.all_gather(both_grads, "ctx", axis=0, tiled=True))
    gain_local = jnp.sum(hidden_grad * normed, axis=0)
    normbias_local = jnp.sum(hidden_grad, axis=0)
    scaled_grad = hidden_grad * norm_gain
    tokens_grad = grad_out.astype(jnp.float32) + inv_std * (
        scaled_grad
        - jnp.mean(scaled_grad, axis=-1, keepdims=True)
        - normed * jnp.mean(scaled_grad * normed, axis=-1, keepdims=True)
    )
    out_grad_sum, in_grad_sum = (
        lax.psum(out_grad_local.astype(jnp.bfloat16), "dp").astype(jnp.float32),
        lax.psum(in_grad_local.astype(jnp.bfloat16), "dp").astype(jnp.float32),
    )
    small_sums = lax.psum(
        (gain_local, normbias_local, qkv_bias_local, out_bias_grad, up_bias_local), ("dp", "ctx")
    )
    limits = clip_limit.astype(jnp.float32)
    factor = limits / jnp.maximum(head_maxima, limits)
    column_scale = jnp.tile(jnp.repeat(jnp.sqrt(factor), head_dim), 2)
    clipped_weight = qkv_weight[:, : 2 * model_width].astype(jnp.float32) * column_scale
    clipped_bias = qkv_bias[: 2 * model_width] * column_scale
    return (
        layer_out.reshape(seq_count, stretch_len, model_width),
        tokens_grad.reshape(seq_count, stretch_len, model_width),
        small_sums[0],
        small_sums[1],
        in_grad_sum[:, :qkv_width],
        small_sums[2],
        out_grad_sum[:own_rows],
        small_sums[3],
        in_grad_sum[:, qkv_width:],
        small_sums[4],
        out_grad_sum[own_rows:],
        small_sums[3],
        head_maxima,
        clipped_weight,
        clipped_bias,
    )


def solution(mesh):
    in_specs = (
        P("dp", "ctx", None),
        P("dp", "ctx"),
        P(),
        P(),
        P("ctx", None),
        P(),
        P("ctx", None),
        P(),
        P("ctx", None),
        P(),
        P("ctx", None),
        P(),
        P(),
        P("dp", "ctx", None),
    )
    out_specs = (
        P("dp", "ctx", None),
        P("dp", "ctx", None),
        P(),
        P(),
        P("ctx", None),
        P(),
        P("ctx", None),
        P(),
        P("ctx", None),
        P(),
        P("ctx", None),
        P(),
        P(),
        P("ctx", None),
        P(),
    )
    return jax.shard_map(
        per_device, mesh=mesh, in_specs=in_specs, out_specs=out_specs, check_vma=False
    )
```

profile of v0, /device:TPU:0, one launch (start us, length us, event | category | flops | bytes accessed | tf_op | source)
XLA Modules:
  0.0 2021.1 jit_solution(2774940545295063979)
XLA Ops:
  7.2 7.0 pad_maximum_fusion
  15.4 5.4 pad_maximum_fusion.1
  22.4 490.3 %all-gather.8.cloned.1.call-done = bf16[2048,14336]{1,0:T(8,128)(2,1)} async-done(((bf16[256,14336]{1,0:T(8,128)(2,1)}), bf16[2048,14336]{1,0:T(8,128)(2,1)}) %all-gather.8.cloned.1.call-update) | async-done | bytes 58720272 | tf_op jit(solution)/shard_map/all_gather | solution.py:122
  512.6 30.2 %fusion.59 = f32[128,14336]{1,0:T(8,128)} fusion(bf16[2048,14336]{1,0:T(8,128)(2,1)} %all-gather.8.cloned.1.call-done, bf16[1,128,2048]{2,1,0:T(8,128)(2,1)S(1)} %copy-done.6, f32[2048]{0:T(1024)S(1)} %copy-done.18, f32[2048]{0:T(1024)S(1)} %copy-done.17, f32[128]{0:T(128)S(1)} %add_rsqrt_fusion, f32[128]{0:T(128)S(1)} %broadcast_multiply_fusion.2), kind=kOutput, calls=%fused_computation.116 | convolution fusion | flops 7517765632 | bytes 66601984 | tf_op jit(solution)/shard_map/dot_general | solution.py:120
  554.5 317.5 %all-gather.14.cloned.1.call-done = bf16[10240,2048]{1,0:T(8,128)(2,1)} async-done(((bf16[1280,2048]{1,0:T(8,128)(2,1)}), bf16[10240,2048]{1,0:T(8,128)(2,1)}) %all-gather.14.cloned.1.call-update) | async-done | bytes 41943056 | tf_op jit(solution)/shard_map/all_gather | solution.py:178
  872.0 19.9 fusion.63
  891.9 4.5 slice.182
  897.8 5.6 copy.56
  906.4 14.1 all-gather.10.cloned.1.call-done
  920.5 3.3 copy.57
  927.0 41.7 %all-gather.12.cloned.1.call-done = bf16[1,1024,2048]{1,2,0:T(8,128)(2,1)} async-done(((bf16[1,128,2048]{1,2,0:T(8,128)(2,1)}), bf16[1,1024,2048]{1,2,0:T(8,128)(2,1)}) %all-gather.12.cloned.1.call-update) | async-done | bytes 4194320 | tf_op jit(solution)/shard_map/all_gather | solution.py:143
  968.6 3.3 copy.58
  975.0 68.7 %while.35 = (s32[]{:T(128)}, f32[1,32,128,64]{2,3,1,0:T(8,128)}, f32[1,32,128]{2,1,0:T(8,128)S(1)}, f32[1,32,128]{2,1,0:T(8,128)S(1)}, s32[8]{0:T(128)S(1)}, /*i...) while((s32[]{:T(128)}, f32[1,32,128,64]{2,3,1,0:T(8,128)}, ...), condition=%wide.region_5.6_spmd.clone, body=%wide.region_2.5_spmd.clone.sunk | while | flops 141861120 | bytes 10291419 | solution.py:159
  1045.3 208.7 %while.36 = (s32[]{:T(128)}, bf16[2,1,128,2048]{2,3,1,0:T(8,128)(2,1)}, f32[2,1,128,2048]{2,3,1,0:T(8,128)}, f32[1,128,32,64]{1,3,2,0:T(8,128)}, s32[]{:T(128)},...) while((s32[]{:T(128)}, ...), condition=%wide.region_8.9_spmd.clone, body=%wide.region_7.8_spmd.clone.sunk | while | flops 343425280 | bytes 50923972 | solution.py:261
  1058.1 10.1 collective-permute-done.1
  1077.3 4.6 collective-permute-start.1
  1081.9 5.5 collective-permute-start
  1102.6 11.4 collective-permute-start.1
  1114.0 5.5 collective-permute-start
  1131.7 14.4 collective-permute-start.1
  1146.1 5.5 collective-permute-start
  1163.9 14.4 collective-permute-start.1
  1178.3 5.5 collective-permute-start
  1196.0 14.4 collective-permute-start.1
  1210.4 5.5 collective-permute-start
  1228.2 14.4 collective-permute-start.1
  1242.6 5.5 collective-permute-start
  1260.5 14.5 collective-permute-start.2
  1275.0 5.0 convert_reduce_fusion
  1287.5 3.5 pad_maximum_fusion.2
  1291.0 3.3 copy.54
  1296.2 12.7 all-to-all-start.1
  1311.0 30.6 %multiply_reduce_fusion = (f32[2048]{0:T(1024)}, f32[128]{0:T(128)S(1)}, f32[128]{0:T(128)S(1)}, f32[2048]{0:T(1024)}, f32[128,2048]{1,0:T(8,128)}) fusion(bf16[1,128,2048]{2,1,0:T(8,128)(2,1)S(1)} %copy-done.7, f32[128]{0:T(128)S(1)} %add_rsqrt_fusion, f32[128]{0:T(128)S(1)} %broadcast_multiply_fusion.2, f32[2048]{0:T(1024)S(1)} %copy-done.17, ...), kind=kOutput, calls=%fused_computation.107 | convolution fusion | flops 7526150144 | bytes 63989760 | tf_op jit(solution)/shard_map/dot_general | solution.py:54
  1341.6 3.5 convert_reduce_fusion.2
  1345.1 99.8 %all-to-all-done.1 = bf16[128,8,1280]{0,2,1:T(8,128)(2,1)S(1)} async-done(((bf16[128,8,1280]{0,2,1:T(8,128)(2,1)}), bf16[128,8,1280]{0,2,1:T(8,128)(2,1)S(1)}, u32[]{:S(2)}, u32[]{:S(2)}) %all-to-all-start.1) | async-done | bytes 2621472 | tf_op jit(solution)/shard_map/all_to_all | solution.py:188
  1444.9 4.1 all-to-all-start
  1451.6 10.0 convolution_convert_fusion.1
  1461.7 18.6 all-to-all-done
  1480.3 138.4 %all-gather.16.cloned.1.call-done = bf16[1024,14336]{1,0:T(8,128)(2,1)} async-done(((bf16[128,14336]{1,0:T(8,128)(2,1)}), bf16[1024,14336]{1,0:T(8,128)(2,1)}) %all-gather.16.cloned.1.call-update) | async-done | bytes 29360144 | tf_op jit(solution)/shard_map/all_gather | solution.py:279
  1618.6 15.4 convolution_convert_fusion
  1634.1 38.1 %pmax.7 = f32[32]{0:T(128)S(1)} all-reduce(f32[32]{0:T(128)S(1)} %get-tuple-element.484), channel_id=1, replica_groups=mesh['dp'=4,'ctx'=8] {'dp','ctx'}, use_global_device_ids=true, to_apply=%region_24.25 | all-reduce | flops 32 | bytes 256 | tf_op jit(solution)/shard_map/pmax | solution.py:163
  1673.0 4.1 convert_multiply_fusion
  1677.1 17.5 fusion.46
  1694.6 52.8 %all-reduce.5.cloned.1.call-done = (f32[2048]{0:T(1024)}, f32[2048]{0:T(1024)}, f32[6144]{0:T(1024)}, f32[2048]{0:T(1024)}, f32[8192]{0:T(1024)}) async-done(((f32[2048]{0:T(1024)}, f32[2048]{0:T(1024)}, f32[6144]{0:T(1024)}, f32[2048]{0:T(1024)}, f32[8192]{0:T(1024)}), (f32[2048]{0:T(1024)}, f32[2048]{0:T(1024)}, f32[6144]{0:T(1024)}, f32[2048]{0:T(1024)}, f32[8192]{0:T(1024)})) %all-reduce.5.cloned.1.call-update) | async-done | bytes 81936 | tf_op jit(solution)/shard_map/psum | solution.py:292
  1747.4 246.5 %all-reduce.7.cloned.1.call-done = (bf16[256,14336]{1,0:T(8,128)(2,1)}, bf16[1280,2048]{1,0:T(8,128)(2,1)}) async-done(((bf16[256,14336]{1,0:T(8,128)(2,1)}, bf16[1280,2048]{1,0:T(8,128)(2,1)}), (bf16[256,14336]{1,0:T(8,128)(2,1)}, bf16[1280,2048]{1,0:T(8,128)(2,1)})) %all-reduce.7.cloned.1.call-update) | async-done | bytes 12582928 | tf_op jit(solution)/shard_map/psum | solution.py:290
  1993.9 6.0 slice.183
  1999.9 4.4 slice.185
  2005.9 4.4 slice.186
  (373 shorter events, 191.7 us)
Async XLA Ops:
  7.2 505.4 %all-gather.8.cloned.1.call-start = ((), (), s32[]{:S(2)}) async-start(), calls=%async_computation.2 | async-start | bytes 66060288 | tf_op jit(solution)/shard_map/all_gather | solution.py:122
  14.2 857.7 %all-gather.14.cloned.1.call-start = ((), (), s32[]{:S(2)}) async-start(), calls=%async_computation.5 | async-start | bytes 47185920 | tf_op jit(solution)/shard_map/all_gather | solution.py:178
  20.8 491.8 %copy-start.17 = (f32[2048]{0:T(1024)S(1)}, f32[2048]{0:T(1024)}, u32[]{:S(2)}) copy-start(f32[2048]{0:T(1024)} %param.20) | copy-start | bytes 24580
  20.8 491.8 %copy-start.18 = (f32[2048]{0:T(1024)S(1)}, f32[2048]{0:T(1024)}, u32[]{:S(2)}) copy-start(f32[2048]{0:T(1024)} %param.21) | copy-start | bytes 24580
  20.9 899.7 %all-gather.10.cloned.1.call-start = ((), (), s32[]{:S(2)}) async-start(), calls=%async_computation.3 | async-start | bytes 4718592 | tf_op jit(solution)/shard_map/all_gather | solution.py:142
  22.3 520.5 %copy-start.19 = (f32[6144]{0:T(1024)S(1)}, f32[6144]{0:T(1024)}, u32[]{:S(2)}) copy-start(f32[6144]{0:T(1024)} %param.23) | copy-start | bytes 73732
  549.9 322.1 %copy-start.14 = (bf16[1,128,2048]{2,1,0:T(8,128)(2,1)S(1)}, bf16[1,128,2048]{2,1,0:T(8,128)(2,1)}, u32[]{:S(2)}) copy-start(bf16[1,128,2048]{2,1,0:T(8,128)(2,1)} %param.31) | copy-start | bytes 1572868
  550.9 417.7 %all-gather.12.cloned.1.call-start = ((), (), s32[]{:S(2)}) async-start(), calls=%async_computation.4 | async-start | bytes 4718592 | tf_op jit(solution)/shard_map/all_gather | solution.py:143
  553.1 898.5 %all-gather.18.cloned.1.call-start = ((), (), s32[]{:S(2)}) async-start(), calls=%async_computation.7 | async-start | bytes 4718592 | tf_op jit(solution)/shard_map/all_gather | solution.py:192
  553.7 1064.9 %all-gather.16.cloned.1.call-start = ((), (), s32[]{:S(2)}) async-start(), calls=%async_computation.6 | async-start | bytes 33030144 | tf_op jit(solution)/shard_map/all_gather | solution.py:279
  1051.9 16.3 collective-permute-start.1
  1052.2 18.7 collective-permute-start
  1077.3 16.3 collective-permute-start.1
  1081.9 14.4 collective-permute-start
  1102.6 20.0 collective-permute-start.1
  1114.0 11.4 collective-permute-start
  1131.7 23.1 %collective-permute-start.1 = (bf16[2,1,128,2048]{2,3,1,0:T(8,128)(2,1)}, bf16[2,1,128,2048]{2,3,1,0:T(8,128)(2,1)}, u32[]{:S(2)}, u32[]{:S(2)}) collective-permute-start(bf16[2,1,128,2048]{2,3,1,0:T(8,128)(2,1)} %fusion.137), channel_id=1, source_target_pairs={{0,1},{1,2},{2,3},{3,4},{4,5},{5,6},{6,7},{7,0},{8,9},{9,10},{10,1... | collective-permute-start | bytes 3145736 | tf_op jit(solution)/shard_map/while/body/eval_jaxpr/ppermute | solution.py:23
  1146.1 11.4 collective-permute-start
  1163.9 23.1 %collective-permute-start.1 = (bf16[2,1,128,2048]{2,3,1,0:T(8,128)(2,1)}, bf16[2,1,128,2048]{2,3,1,0:T(8,128)(2,1)}, u32[]{:S(2)}, u32[]{:S(2)}) collective-permute-start(bf16[2,1,128,2048]{2,3,1,0:T(8,128)(2,1)} %fusion.137), channel_id=1, source_target_pairs={{0,1},{1,2},{2,3},{3,4},{4,5},{5,6},{6,7},{7,0},{8,9},{9,10},{10,1... | collective-permute-start | bytes 3145736 | tf_op jit(solution)/shard_map/while/body/eval_jaxpr/ppermute | solution.py:23
  1178.3 11.4 collective-permute-start
  1196.0 23.1 %collective-permute-start.1 = (bf16[2,1,128,2048]{2,3,1,0:T(8,128)(2,1)}, bf16[2,1,128,2048]{2,3,1,0:T(8,128)(2,1)}, u32[]{:S(2)}, u32[]{:S(2)}) collective-permute-start(bf16[2,1,128,2048]{2,3,1,0:T(8,128)(2,1)} %fusion.137), channel_id=1, source_target_pairs={{0,1},{1,2},{2,3},{3,4},{4,5},{5,6},{6,7},{7,0},{8,9},{9,10},{10,1... | collective-permute-start | bytes 3145736 | tf_op jit(solution)/shard_map/while/body/eval_jaxpr/ppermute | solution.py:23
  1210.4 11.4 collective-permute-start
  1228.2 23.1 %collective-permute-start.1 = (bf16[2,1,128,2048]{2,3,1,0:T(8,128)(2,1)}, bf16[2,1,128,2048]{2,3,1,0:T(8,128)(2,1)}, u32[]{:S(2)}, u32[]{:S(2)}) collective-permute-start(bf16[2,1,128,2048]{2,3,1,0:T(8,128)(2,1)} %fusion.137), channel_id=1, source_target_pairs={{0,1},{1,2},{2,3},{3,4},{4,5},{5,6},{6,7},{7,0},{8,9},{9,10},{10,1... | collective-permute-start | bytes 3145736 | tf_op jit(solution)/shard_map/while/body/eval_jaxpr/ppermute | solution.py:23
  1242.6 11.4 collective-permute-start
  1257.3 17.8 slice-start
  1258.8 16.2 slice-start.1
  1259.2 15.8 copy-start.8
  1259.2 15.8 copy-start.21
  1260.5 19.5 copy-start.4
  1260.5 20.4 %collective-permute-start.2 = (bf16[2,1,128,2048]{2,3,1,0:T(8,128)(2,1)S(1)}, bf16[2,1,128,2048]{2,3,1,0:T(8,128)(2,1)S(1)}, u32[]{:S(2)}, u32[]{:S(2)}) collective-permute-start(bf16[2,1,128,2048]{2,3,1,0:T(8,128)(2,1)S(1)} %fusion.47), channel_id=1, source_target_pairs={{0,1},{1,2},{2,3},{3,4},{4,5},{5,6},{6,7},{7,0},{8,9},{9,10},{10,1... | collective-permute-start | bytes 3145736 | tf_op jit(solution)/shard_map/ppermute | solution.py:23
  1280.1 7.4 copy-start.9
  1296.2 12.7 copy-start.7
  1296.2 148.7 %all-to-all-start.1 = ((bf16[128,8,1280]{0,2,1:T(8,128)(2,1)}), bf16[128,8,1280]{0,2,1:T(8,128)(2,1)S(1)}, u32[]{:S(2)}, u32[]{:S(2)}) async-start(bf16[128,8,1280]{0,2,1:T(8,128)(2,1)} %pad_maximum_fusion.3), calls=%async_computation.1 | async-start | bytes 5242880 | tf_op jit(solution)/shard_map/all_to_all | solution.py:188
  1308.8 438.6 %all-reduce.5.cloned.1.call-start = ((), (), s32[]{:S(2)}) async-start(), calls=%async_computation.8 | async-start | bytes 163840 | tf_op jit(solution)/shard_map/psum | solution.py:292
  1444.9 35.4 %all-to-all-start = ((bf16[128,8,256]{2,0,1:T(8,128)(2,1)}), bf16[128,8,256]{2,0,1:T(8,128)(2,1)}, u32[]{:S(2)}, u32[]{:S(2)}) async-start(bf16[128,8,256]{2,0,1:T(8,128)(2,1)} %fusion.55), calls=%async_computation | async-start | bytes 1048576 | tf_op jit(solution)/shard_map/all_to_all | solution.py:189
  1449.0 544.9 %all-reduce.7.cloned.1.call-start = ((), (), s32[]{:S(2)}) async-start(), calls=%async_computation.9 | async-start | bytes 25165824 | tf_op jit(solution)/shard_map/psum | solution.py:290
  1634.0 38.2 %copy-start.30 = (s32[32]{0:T(128)S(1)}, s32[32]{0:T(128)}, u32[]{:S(2)}) copy-start(s32[32]{0:T(128)} %param.30) | copy-start | bytes 388
  1634.0 38.3 %copy-start.20 = (f32[6144]{0:T(1024)S(1)}, f32[6144]{0:T(1024)}, u32[]{:S(2)}) copy-start(f32[6144]{0:T(1024)} %param.23) | copy-start | bytes 73732
  1672.2 5.0 copy-start.31
  1673.0 4.2 copy-start.28
  1993.9 6.0 copy-start.5
  1993.9 10.4 slice-start.2
  1999.9 4.4 slice-start.3
  2005.9 4.5 copy-start.23
  2005.9 5.1 copy-start.26
  2005.9 5.7 copy-start.25
  2005.9 6.3 copy-start.24
  2005.9 7.5 copy-start.22
  (32 other events, 50.3 us)
Sparse Core Ops, SparseCore 0:
  14.4 498.2 all-gather.7
  514.8 357.0 all-gather.13
  874.1 46.3 all-gather.9
  922.5 46.0 all-gather.11
  970.1 45.3 all-gather.17
  1291.1 327.4 all-gather.15
  1626.2 121.1 all-reduce.4
  1752.3 241.5 all-reduce.6
where the time goes:
time: 2030 us; the launch traced here: 2020 us
  waiting for transfers between devices  1430 us (70%)
  matrix products  208 us (10%)
  starting transfers between devices  142 us (7%)
  local copies, waits for them, and re-layouts  86.2 us (4%)
  other arithmetic  76.7 us (4%)
  blocking collectives  38.1 us (2%)
  loops' own time  21.9 us (1%)
    all_gather x1, waiting for transfers between devices, per_device(): lax.all_gather(in_local, 'ctx', axis=0, tiled=True)  490 us
    all_gather x1, waiting for transfers between devices, per_device(): lax.all_gather(out_local, 'ctx', axis=0, tiled=True)  317 us
    psum x1, waiting for transfers between devices, per_device(): lax.psum(in_grad_local.astype(jnp.bfloat16), 'dp').astype(jnp.float32)  247 us
    all_gather x1, waiting for transfers between devices, per_device(): lax.all_gather(both_grads, 'ctx', axis=0, tiled=True)  138 us
    all_to_all x1, waiting for transfers between devices, per_device(): lax.all_to_all(left_stack, 'ctx', split_axis=1, concat_axis=0, tiled=True)  99.8 us
    ppermute x8, starting transfers between devices, from_behind_2(): return lax.ppermute(value, axis, pairs)  88.4 us
    psum x1, waiting for transfers between devices, per_device(): lax.psum((gain_local, normbias_local, qkv_bias_local, out_bias_grad, up_b...  52.8 us
    dot_general x2, matrix products, contract_last(): lax.dot_general(left, right, (((1,), (1,)), no_batch), preferred_element_...  50.5 us
  transfers between devices with their start and end apart: 25, of which 11 were waited for; matrix products, arithmetic and copies ran while one was open for 17% of the time, Pallas kernels for 0%

commit v1 on v0

--- a/solution.py
+++ b/solution.py
@@ -9,6 +9,24 @@
 masked_score = -1e30
 rope_base = 10000.0
 no_batch = ((), ())
+
+
+def ring_gather(value, axis, dim):
+    ways, here, step = (lax.axis_size(axis), lax.axis_index(axis), value.shape[dim])
+    lengths = [n * ways if d == dim else n for d, n in enumerate(value.shape)]
+    full = lax.dynamic_update_slice_in_dim(
+        jnp.zeros(lengths, value.dtype), value, here * step, axis=dim
+    )
+    going_up = going_down = value
+    for far in range(1, ways // 2 + 1):
+        going_up = lax.ppermute(going_up, axis, [(d, (d + 1) % ways) for d in range(ways)])
+        full = lax.dynamic_update_slice_in_dim(full, going_up, (here - far) % ways * step, axis=dim)
+        if 2 * far < ways:
+            going_down = lax.ppermute(going_down, axis, [(d, (d - 1) % ways) for d in range(ways)])
+            full = lax.dynamic_update_slice_in_dim(
+                full, going_down, (here + far) % ways * step, axis=dim
+            )
+    return full
 
 
 def from_behind(value, axis, steps):
@@ -276,7 +294,7 @@
     both_grads = jnp.concatenate([joined_low, up_grad_rows], axis=1)
     hidden_grad = contract_last(both_grads, lax.all_gather(in_local, "ctx", axis=0, tiled=True))
     columns = hidden_owned
-    in_grad_local = contract_first(columns, lax.all_gather(both_grads, "ctx", axis=0, tiled=True))
+    in_grad_local = contract_first(columns, ring_gather(both_grads, "ctx", 0))
     gain_local = jnp.sum(hidden_grad * normed, axis=0)
     normbias_local = jnp.sum(hidden_grad, axis=0)
     scaled_grad = hidden_grad * norm_gain

time: 2030 us -> 1950 us (0.961)
  waiting for transfers between devices: 1430 us -> 1200 us
  starting transfers between devices: 142 us -> 240 us
  local copies, waits for them, and re-layouts: 86.2 us -> 118 us
  blocking collectives: 38.1 us -> 66.2 us
    ppermute x0 -> x7, waiting for transfers between devices: none -> 146 us  [the longest x3 91.3 us: ring_gather(): lax.ppermute(going_down, axis, [(d, (d - 1) % ways) for d in range(ways)])]
    all_gather x1 -> x0, waiting for transfers between devices: 138 us -> none  [per_device(): lax.all_gather(both_grads, 'ctx', axis=0, tiled=True)]
    all_to_all x1, waiting for transfers between devices: 99.8 us -> 0.01 us  [per_device(): lax.all_to_all(left_stack, 'ctx', split_axis=1, concat_axis=0, tiled=True)]
    ppermute x0 -> x7, starting transfers between devices: none -> 71.1 us  [the longest x4 60.4 us: ring_gather(): lax.ppermute(going_up, axis, [(d, (d + 1) % ways) for d in range(ways)])]
    psum x1, waiting for transfers between devices: 247 us -> 177 us  [per_device(): lax.psum(in_grad_local.astype(jnp.bfloat16), 'dp').astype(jnp.float32)]
    psum x1, waiting for transfers between devices: 52.8 us -> 0.01 us  [per_device(): lax.psum((gain_local, normbias_local, qkv_bias_local, out_bias_grad, up_b...]
    all_to_all x1, starting transfers between devices: 4.14 us -> 39.2 us  [per_device(): lax.all_to_all(hidden, 'ctx', split_axis=1, concat_axis=0, tiled=True)]
    pmax x1, blocking collectives: 38.1 us -> 66.2 us  [per_device(): head_maxima = lax.pmax(jnp.max(row_max, axis=(0, 2)), ('dp', 'ctx'))]
  transfers between devices with their start and end apart: 25 -> 31, of which waited for: 11 -> 13; matrix products, arithmetic and copies ran while one was open for 17% -> 19% of each run, Pallas kernels for 0% -> 0%
where the time goes in v1:
time: 1950 us
  waiting for transfers between devices  1200 us (62%)
  starting transfers between devices  240 us (12%)
  matrix products  207 us (11%)
  local copies, waits for them, and re-layouts  118 us (6%)
  other arithmetic  77.7 us (4%)
  blocking collectives  66.2 us (3%)
  loops' own time  21.9 us (1%)
    all_gather x1, waiting for transfers between devices, per_device(): lax.all_gather(in_local, 'ctx', axis=0, tiled=True)  490 us
    all_gather x1, waiting for transfers between devices, per_device(): lax.all_gather(out_local, 'ctx', axis=0, tiled=True)  318 us
    psum x1, waiting for transfers between devices, per_device(): lax.psum(in_grad_local.astype(jnp.bfloat16), 'dp').astype(jnp.float32)  177 us
    ppermute x3, waiting for transfers between devices, ring_gather(): lax.ppermute(going_down, axis, [(d, (d - 1) % ways) for d in range(ways)])  91.3 us
    ppermute x8, starting transfers between devices, from_behind_2(): return lax.ppermute(value, axis, pairs)  88.5 us
    pmax x1, blocking collectives, per_device(): head_maxima = lax.pmax(jnp.max(row_max, axis=(0, 2)), ('dp', 'ctx'))  66.2 us
    ppermute x4, starting transfers between devices, ring_gather(): lax.ppermute(going_up, axis, [(d, (d + 1) % ways) for d in range(ways)])  60.4 us
    ppermute x4, waiting for transfers between devices, ring_gather(): lax.ppermute(going_up, axis, [(d, (d + 1) % ways) for d in range(ways)])  54.3 us
  transfers between devices with their start and end apart: 31, of which 13 were waited for; matrix products, arithmetic and copies ran while one was open for 19% of the time, Pallas kernels for 0%

profile of v1, /device:TPU:0, one launch (start us, length us, event | category | flops | bytes accessed | tf_op | source)
XLA Modules:
  0.0 1945.7 jit_solution(15188259725968050786)
XLA Ops:
  7.2 7.0 pad_maximum_fusion
  15.4 5.4 pad_maximum_fusion.1
  22.4 490.3 %all-gather.7.cloned.1.call-done = bf16[2048,14336]{1,0:T(8,128)(2,1)} async-done(((bf16[256,14336]{1,0:T(8,128)(2,1)}), bf16[2048,14336]{1,0:T(8,128)(2,1)}) %all-gather.7.cloned.1.call-update) | async-done | bytes 58720272 | tf_op jit(solution)/shard_map/all_gather | solution.py:140
  512.6 30.2 %fusion.59 = f32[128,14336]{1,0:T(8,128)} fusion(bf16[2048,14336]{1,0:T(8,128)(2,1)} %all-gather.7.cloned.1.call-done, bf16[1,128,2048]{2,1,0:T(8,128)(2,1)S(1)} %copy-done.6, f32[2048]{0:T(1024)S(1)} %copy-done.18, f32[2048]{0:T(1024)S(1)} %copy-done.17, f32[128]{0:T(128)S(1)} %add_rsqrt_fusion, f32[128]{0:T(128)S(1)} %broadcast_multiply_fusion.2), kind=kOutput, calls=%fused_computation.116 | convolution fusion | flops 7517765632 | bytes 66601984 | tf_op jit(solution)/shard_map/dot_general | solution.py:138
  553.9 318.0 %all-gather.13.cloned.1.call-done = bf16[10240,2048]{1,0:T(8,128)(2,1)} async-done(((bf16[1280,2048]{1,0:T(8,128)(2,1)}), bf16[10240,2048]{1,0:T(8,128)(2,1)}) %all-gather.13.cloned.1.call-update) | async-done | bytes 41943056 | tf_op jit(solution)/shard_map/all_gather | solution.py:196
  872.0 19.9 %fusion.63 = f32[10240,128]{1,0:T(8,128)} fusion(bf16[10240,2048]{1,0:T(8,128)(2,1)} %all-gather.13.cloned.1.call-done, bf16[1,128,2048]{2,1,0:T(8,128)(2,1)S(1)} %copy-done.14), kind=kOutput, calls=%fused_computation.129 | convolution fusion | flops 5368709120 | bytes 47710208 | tf_op jit(solution)/shard_map/dot_general | solution.py:72
  891.9 4.5 slice.182
  897.8 5.6 copy.56
  906.4 14.2 all-gather.9.cloned.1.call-done
  927.0 41.7 %all-gather.11.cloned.1.call-done = bf16[1,1024,2048]{1,2,0:T(8,128)(2,1)} async-done(((bf16[1,128,2048]{1,2,0:T(8,128)(2,1)}), bf16[1,1024,2048]{1,2,0:T(8,128)(2,1)}) %all-gather.11.cloned.1.call-update) | async-done | bytes 4194320 | tf_op jit(solution)/shard_map/all_gather | solution.py:161
  975.0 68.7 %while.35 = (s32[]{:T(128)}, f32[1,32,128,64]{2,3,1,0:T(8,128)}, f32[1,32,128]{2,1,0:T(8,128)S(1)}, f32[1,32,128]{2,1,0:T(8,128)S(1)}, s32[8]{0:T(128)S(1)}, /*i...) while((s32[]{:T(128)}, f32[1,32,128,64]{2,3,1,0:T(8,128)}, ...), condition=%wide.region_5.6_spmd.clone, body=%wide.region_2.5_spmd.clone.sunk | while | flops 141861120 | bytes 10291419 | solution.py:177
  1045.3 208.6 %while.36 = (s32[]{:T(128)}, bf16[2,1,128,2048]{2,3,1,0:T(8,128)(2,1)}, f32[2,1,128,2048]{2,3,1,0:T(8,128)}, f32[1,128,32,64]{1,3,2,0:T(8,128)}, s32[]{:T(128)},...) while((s32[]{:T(128)}, ...), condition=%wide.region_8.9_spmd.clone, body=%wide.region_7.8_spmd.clone.sunk | while | flops 343425280 | bytes 50923972 | solution.py:279
  1058.0 10.2 collective-permute-done.1
  1077.2 4.6 collective-permute-start.1
  1081.8 5.4 collective-permute-start
  1102.6 11.4 collective-permute-start.1
  1114.0 5.4 collective-permute-start
  1131.7 14.4 collective-permute-start.1
  1146.1 5.4 collective-permute-start
  1163.8 14.4 collective-permute-start.1
  1178.2 5.4 collective-permute-start
  1196.0 14.4 collective-permute-start.1
  1210.4 5.4 collective-permute-start
  1228.1 14.4 collective-permute-start.1
  1242.5 5.4 collective-permute-start
  1259.7 14.5 collective-permute-start.2
  1274.2 5.0 convert_reduce_fusion
  1285.4 10.0 broadcast_in_dim.103
  1298.8 8.4 collective-permute-start.3
  1312.3 4.5 all-to-all-start.1
  1324.8 39.2 %collective-permute-done.3 = bf16[128,14336]{1,0:T(8,128)(2,1)} collective-permute-done((bf16[128,14336]{1,0:T(8,128)(2,1)}, bf16[128,14336]{1,0:T(8,128)(2,1)}, u32[]{:S(2)}, u32[]{:S(2)}) %collective-permute-start.3) | collective-permute-done | bytes 3670048 | tf_op jit(solution)/shard_map/ppermute | solution.py:22
  1364.0 17.3 collective-permute-start.5
  1381.3 27.9 %multiply_reduce_fusion = (f32[2048]{0:T(1024)}, f32[128]{0:T(128)S(1)}, f32[128]{0:T(128)S(1)}, f32[2048]{0:T(1024)}, f32[128,2048]{1,0:T(8,128)}) fusion(bf16[1,128,2048]{2,1,0:T(8,128)(2,1)S(1)} %copy-done.7, f32[128]{0:T(128)S(1)} %add_rsqrt_fusion, f32[128]{0:T(128)S(1)} %broadcast_multiply_fusion.2, f32[2048]{0:T(1024)S(1)} %copy-done.17, ...), kind=kOutput, calls=%fused_computation.107 | convolution fusion | flops 7526150144 | bytes 63989760 | tf_op jit(solution)/shard_map/dot_general | solution.py:72
  1412.8 39.2 %all-to-all-start = ((bf16[128,8,256]{2,0,1:T(8,128)(2,1)}), bf16[128,8,256]{2,0,1:T(8,128)(2,1)}, u32[]{:S(2)}, u32[]{:S(2)}) async-start(bf16[128,8,256]{2,0,1:T(8,128)(2,1)} %fusion.55), calls=%async_computation | async-start | bytes 1048576 | tf_op jit(solution)/shard_map/all_to_all | solution.py:207
  1458.1 10.0 convolution_convert_fusion.1
  1471.0 17.6 collective-permute-start.7
  1497.1 45.6 %collective-permute-done.6 = bf16[128,14336]{1,0:T(8,128)(2,1)} collective-permute-done((bf16[128,14336]{1,0:T(8,128)(2,1)}, bf16[128,14336]{1,0:T(8,128)(2,1)}, u32[]{:S(2)}, u32[]{:S(2)}) %collective-permute-start.6) | collective-permute-done | bytes 3670048 | tf_op jit(solution)/shard_map/ppermute | solution.py:25
  1550.5 5.9 collective-permute-done.7
  1556.4 17.1 collective-permute-start.9
  1579.8 45.7 %collective-permute-done.8 = bf16[128,14336]{1,0:T(8,128)(2,1)S(1)} collective-permute-done((bf16[128,14336]{1,0:T(8,128)(2,1)}, bf16[128,14336]{1,0:T(8,128)(2,1)S(1)}, u32[]{:S(2)}, u32[]{:S(2)}) %collective-permute-start.8) | collective-permute-done | bytes 3670048 | tf_op jit(solution)/shard_map/ppermute | solution.py:25
  1627.7 6.2 collective-permute-done.9
  1636.0 15.6 convolution_convert_fusion
  1651.7 66.2 %pmax.7 = f32[32]{0:T(128)S(1)} all-reduce(f32[32]{0:T(128)S(1)} %get-tuple-element.486), channel_id=1, replica_groups=mesh['dp'=4,'ctx'=8] {'dp','ctx'}, use_global_device_ids=true, to_apply=%region_24.25 | all-reduce | flops 32 | bytes 256 | tf_op jit(solution)/shard_map/pmax | solution.py:181
  1722.8 18.6 fusion.46
  1741.4 177.2 %all-reduce.7.cloned.1.call-done = (bf16[256,14336]{1,0:T(8,128)(2,1)}, bf16[1280,2048]{1,0:T(8,128)(2,1)}) async-done(((bf16[256,14336]{1,0:T(8,128)(2,1)}, bf16[1280,2048]{1,0:T(8,128)(2,1)}), (bf16[256,14336]{1,0:T(8,128)(2,1)}, bf16[1280,2048]{1,0:T(8,128)(2,1)})) %all-reduce.7.cloned.1.call-update) | async-done | bytes 12582928 | tf_op jit(solution)/shard_map/psum | solution.py:308
  1918.6 6.0 slice.183
  1924.5 4.4 slice.185
  1930.5 4.4 slice.186
  (391 shorter events, 249.1 us)
Async XLA Ops:
  7.2 505.4 %all-gather.7.cloned.1.call-start = ((), (), s32[]{:S(2)}) async-start(), calls=%async_computation.2 | async-start | bytes 66060288 | tf_op jit(solution)/shard_map/all_gather | solution.py:140
  14.2 857.7 %all-gather.13.cloned.1.call-start = ((), (), s32[]{:S(2)}) async-start(), calls=%async_computation.5 | async-start | bytes 47185920 | tf_op jit(solution)/shard_map/all_gather | solution.py:196
  20.8 491.8 %copy-start.17 = (f32[2048]{0:T(1024)S(1)}, f32[2048]{0:T(1024)}, u32[]{:S(2)}) copy-start(f32[2048]{0:T(1024)} %param.20) | copy-start | bytes 24580
  20.8 491.8 %copy-start.18 = (f32[2048]{0:T(1024)S(1)}, f32[2048]{0:T(1024)}, u32[]{:S(2)}) copy-start(f32[2048]{0:T(1024)} %param.21) | copy-start | bytes 24580
  20.9 899.7 %all-gather.9.cloned.1.call-start = ((), (), s32[]{:S(2)}) async-start(), calls=%async_computation.3 | async-start | bytes 4718592 | tf_op jit(solution)/shard_map/all_gather | solution.py:160
  22.3 520.5 %copy-start.19 = (f32[6144]{0:T(1024)S(1)}, f32[6144]{0:T(1024)}, u32[]{:S(2)}) copy-start(f32[6144]{0:T(1024)} %param.23) | copy-start | bytes 73732
  549.1 322.8 %copy-start.14 = (bf16[1,128,2048]{2,1,0:T(8,128)(2,1)S(1)}, bf16[1,128,2048]{2,1,0:T(8,128)(2,1)}, u32[]{:S(2)}) copy-start(bf16[1,128,2048]{2,1,0:T(8,128)(2,1)} %param.31) | copy-start | bytes 1572868
  551.0 417.7 %all-gather.11.cloned.1.call-start = ((), (), s32[]{:S(2)}) async-start(), calls=%async_computation.4 | async-start | bytes 4718592 | tf_op jit(solution)/shard_map/all_gather | solution.py:161
  553.1 904.9 %all-gather.15.cloned.1.call-start = ((), (), s32[]{:S(2)}) async-start(), calls=%async_computation.6 | async-start | bytes 4718592 | tf_op jit(solution)/shard_map/all_gather | solution.py:210
  1051.9 16.3 collective-permute-start.1
  1052.2 18.7 collective-permute-start
  1077.2 16.3 collective-permute-start.1
  1081.8 14.4 collective-permute-start
  1102.6 20.0 %collective-permute-start.1 = (bf16[2,1,128,2048]{2,3,1,0:T(8,128)(2,1)}, bf16[2,1,128,2048]{2,3,1,0:T(8,128)(2,1)}, u32[]{:S(2)}, u32[]{:S(2)}) collective-permute-start(bf16[2,1,128,2048]{2,3,1,0:T(8,128)(2,1)} %fusion.137), channel_id=1, source_target_pairs={{0,1},{1,2},{2,3},{3,4},{4,5},{5,6},{6,7},{7,0},{8,9},{9,10},{10,1... | collective-permute-start | bytes 3145736 | tf_op jit(solution)/shard_map/while/body/eval_jaxpr/ppermute | solution.py:41
  1114.0 11.4 collective-permute-start
  1131.7 23.1 %collective-permute-start.1 = (bf16[2,1,128,2048]{2,3,1,0:T(8,128)(2,1)}, bf16[2,1,128,2048]{2,3,1,0:T(8,128)(2,1)}, u32[]{:S(2)}, u32[]{:S(2)}) collective-permute-start(bf16[2,1,128,2048]{2,3,1,0:T(8,128)(2,1)} %fusion.137), channel_id=1, source_target_pairs={{0,1},{1,2},{2,3},{3,4},{4,5},{5,6},{6,7},{7,0},{8,9},{9,10},{10,1... | collective-permute-start | bytes 3145736 | tf_op jit(solution)/shard_map/while/body/eval_jaxpr/ppermute | solution.py:41
  1146.1 11.4 collective-permute-start
  1163.8 23.1 %collective-permute-start.1 = (bf16[2,1,128,2048]{2,3,1,0:T(8,128)(2,1)}, bf16[2,1,128,2048]{2,3,1,0:T(8,128)(2,1)}, u32[]{:S(2)}, u32[]{:S(2)}) collective-permute-start(bf16[2,1,128,2048]{2,3,1,0:T(8,128)(2,1)} %fusion.137), channel_id=1, source_target_pairs={{0,1},{1,2},{2,3},{3,4},{4,5},{5,6},{6,7},{7,0},{8,9},{9,10},{10,1... | collective-permute-start | bytes 3145736 | tf_op jit(solution)/shard_map/while/body/eval_jaxpr/ppermute | solution.py:41
  1178.2 11.4 collective-permute-start
  1196.0 23.1 %collective-permute-start.1 = (bf16[2,1,128,2048]{2,3,1,0:T(8,128)(2,1)}, bf16[2,1,128,2048]{2,3,1,0:T(8,128)(2,1)}, u32[]{:S(2)}, u32[]{:S(2)}) collective-permute-start(bf16[2,1,128,2048]{2,3,1,0:T(8,128)(2,1)} %fusion.137), channel_id=1, source_target_pairs={{0,1},{1,2},{2,3},{3,4},{4,5},{5,6},{6,7},{7,0},{8,9},{9,10},{10,1... | collective-permute-start | bytes 3145736 | tf_op jit(solution)/shard_map/while/body/eval_jaxpr/ppermute | solution.py:41
  1210.4 11.4 collective-permute-start
  1228.1 23.1 %collective-permute-start.1 = (bf16[2,1,128,2048]{2,3,1,0:T(8,128)(2,1)}, bf16[2,1,128,2048]{2,3,1,0:T(8,128)(2,1)}, u32[]{:S(2)}, u32[]{:S(2)}) collective-permute-start(bf16[2,1,128,2048]{2,3,1,0:T(8,128)(2,1)} %fusion.137), channel_id=1, source_target_pairs={{0,1},{1,2},{2,3},{3,4},{4,5},{5,6},{6,7},{7,0},{8,9},{9,10},{10,1... | collective-permute-start | bytes 3145736 | tf_op jit(solution)/shard_map/while/body/eval_jaxpr/ppermute | solution.py:41
  1242.5 11.4 collective-permute-start
  1257.2 17.0 slice-start
  1257.6 16.6 slice-start.1
  1258.7 15.5 copy-start.8
  1258.7 15.5 copy-start.21
  1259.7 19.6 %copy-start.4 = (f32[1,128,32,64]{1,3,2,0:T(8,128)S(1)}, f32[1,128,32,64]{1,3,2,0:T(8,128)}, u32[]{:S(2)}) copy-start(f32[1,128,32,64]{1,3,2,0:T(8,128)} %get-tuple-element.312) | copy-start | bytes 3145732
  1259.7 20.4 %collective-permute-start.2 = (bf16[2,1,128,2048]{2,3,1,0:T(8,128)(2,1)S(1)}, bf16[2,1,128,2048]{2,3,1,0:T(8,128)(2,1)S(1)}, u32[]{:S(2)}, u32[]{:S(2)}) collective-permute-start(bf16[2,1,128,2048]{2,3,1,0:T(8,128)(2,1)S(1)} %fusion.47), channel_id=1, source_target_pairs={{0,1},{1,2},{2,3},{3,4},{4,5},{5,6},{6,7},{7,0},{8,9},{9,10},{10,1... | collective-permute-start | bytes 3145736 | tf_op jit(solution)/shard_map/ppermute | solution.py:41
  1279.3 16.1 copy-start.9
  1298.8 11.6 copy-start.13
  1298.8 65.2 %collective-permute-start.3 = (bf16[128,14336]{1,0:T(8,128)(2,1)}, bf16[128,14336]{1,0:T(8,128)(2,1)}, u32[]{:S(2)}, u32[]{:S(2)}) collective-permute-start(bf16[128,14336]{1,0:T(8,128)(2,1)} %get-tuple-element.464), channel_id=1, source_target_pairs={{0,1},{1,2},{2,3},{3,4},{4,5},{5,6},{6,7},{7,0},{8,9},{9,10},{10,1... | collective-permute-start | bytes 11010056 | tf_op jit(solution)/shard_map/ppermute | solution.py:22
  1312.3 100.5 %all-to-all-start.1 = ((bf16[128,8,1280]{0,2,1:T(8,128)(2,1)}), bf16[128,8,1280]{0,2,1:T(8,128)(2,1)S(1)}, u32[]{:S(2)}, u32[]{:S(2)}) async-start(bf16[128,8,1280]{0,2,1:T(8,128)(2,1)} %pad_maximum_fusion.3), calls=%async_computation.1 | async-start | bytes 5242880 | tf_op jit(solution)/shard_map/all_to_all | solution.py:206
  1316.8 424.5 %all-reduce.5.cloned.1.call-start = ((), (), s32[]{:S(2)}) async-start(), calls=%async_computation.7 | async-start | bytes 163840 | tf_op jit(solution)/shard_map/psum | solution.py:310
  1318.1 136.4 %collective-permute-start.4 = (bf16[128,14336]{1,0:T(8,128)(2,1)}, bf16[128,14336]{1,0:T(8,128)(2,1)}, u32[]{:S(2)}, u32[]{:S(2)}) collective-permute-start(bf16[128,14336]{1,0:T(8,128)(2,1)} %get-tuple-element.464), channel_id=1, source_target_pairs={{0,7},{1,0},{2,1},{3,2},{4,3},{5,4},{6,5},{7,6},{8,15},{9,8},{10,9... | collective-permute-start | bytes 11010056 | tf_op jit(solution)/shard_map/ppermute | solution.py:25
  1364.0 107.0 %collective-permute-start.5 = (bf16[128,14336]{1,0:T(8,128)(2,1)}, bf16[128,14336]{1,0:T(8,128)(2,1)}, u32[]{:S(2)}, u32[]{:S(2)}) collective-permute-start(bf16[128,14336]{1,0:T(8,128)(2,1)} %collective-permute-done.3), channel_id=1, source_target_pairs={{0,1},{1,2},{2,3},{3,4},{4,5},{5,6},{6,7},{7,0},{8,9},{9,10},{10,1... | collective-permute-start | bytes 11010056 | tf_op jit(solution)/shard_map/ppermute | solution.py:22
  1412.8 223.2 %all-to-all-start = ((bf16[128,8,256]{2,0,1:T(8,128)(2,1)}), bf16[128,8,256]{2,0,1:T(8,128)(2,1)}, u32[]{:S(2)}, u32[]{:S(2)}) async-start(bf16[128,8,256]{2,0,1:T(8,128)(2,1)} %fusion.55), calls=%async_computation | async-start | bytes 1048576 | tf_op jit(solution)/shard_map/all_to_all | solution.py:207
  1451.9 466.6 %all-reduce.7.cloned.1.call-start = ((), (), s32[]{:S(2)}) async-start(), calls=%async_computation.8 | async-start | bytes 25165824 | tf_op jit(solution)/shard_map/psum | solution.py:308
  1454.5 88.1 %collective-permute-start.6 = (bf16[128,14336]{1,0:T(8,128)(2,1)}, bf16[128,14336]{1,0:T(8,128)(2,1)}, u32[]{:S(2)}, u32[]{:S(2)}) collective-permute-start(bf16[128,14336]{1,0:T(8,128)(2,1)} %collective-permute-done.4), channel_id=1, source_target_pairs={{0,7},{1,0},{2,1},{3,2},{4,3},{5,4},{6,5},{7,6},{8,15},{9,8},{10,9... | collective-permute-start | bytes 11010056 | tf_op jit(solution)/shard_map/ppermute | solution.py:25
  1471.0 85.4 %collective-permute-start.7 = (bf16[128,14336]{1,0:T(8,128)(2,1)}, bf16[128,14336]{1,0:T(8,128)(2,1)S(1)}, u32[]{:S(2)}, u32[]{:S(2)}) collective-permute-start(bf16[128,14336]{1,0:T(8,128)(2,1)} %collective-permute-done.5), channel_id=1, source_target_pairs={{0,1},{1,2},{2,3},{3,4},{4,5},{5,6},{6,7},{7,0},{8,9},{9,10},{10,1... | collective-permute-start | bytes 11010056 | tf_op jit(solution)/shard_map/ppermute | solution.py:22
  1542.7 82.8 %collective-permute-start.8 = (bf16[128,14336]{1,0:T(8,128)(2,1)}, bf16[128,14336]{1,0:T(8,128)(2,1)S(1)}, u32[]{:S(2)}, u32[]{:S(2)}) collective-permute-start(bf16[128,14336]{1,0:T(8,128)(2,1)} %collective-permute-done.6), channel_id=1, source_target_pairs={{0,7},{1,0},{2,1},{3,2},{4,3},{5,4},{6,5},{7,6},{8,15},{9,8},{10,9... | collective-permute-start | bytes 11010056 | tf_op jit(solution)/shard_map/ppermute | solution.py:25
  1556.4 77.4 %collective-permute-start.9 = (bf16[128,14336]{1,0:T(8,128)(2,1)S(1)}, bf16[128,14336]{1,0:T(8,128)(2,1)S(1)}, u32[]{:S(2)}, u32[]{:S(2)}) collective-permute-start(bf16[128,14336]{1,0:T(8,128)(2,1)S(1)} %collective-permute-done.7), channel_id=1, source_target_pairs={{0,1},{1,2},{2,3},{3,4},{4,5},{5,6},{6,7},{7,0},{8,9},{9,10},{10,1... | collective-permute-start | bytes 11010056 | tf_op jit(solution)/shard_map/ppermute | solution.py:22
  1651.6 66.2 %copy-start.30 = (s32[32]{0:T(128)S(1)}, s32[32]{0:T(128)}, u32[]{:S(2)}) copy-start(s32[32]{0:T(128)} %param.30) | copy-start | bytes 388
  1651.6 66.4 %copy-start.20 = (f32[6144]{0:T(1024)S(1)}, f32[6144]{0:T(1024)}, u32[]{:S(2)}) copy-start(f32[6144]{0:T(1024)} %param.23) | copy-start | bytes 73732
  1651.6 71.1 %copy-start.27 = (f32[2048]{0:T(1024)S(1)}, f32[2048]{0:T(1024)}, u32[]{:S(2)}) copy-start(f32[2048]{0:T(1024)} %param.29) | copy-start | bytes 24580
  1651.7 71.1 %copy-start.28 = (f32[2048]{0:T(1024)S(1)}, f32[2048]{0:T(1024)}, u32[]{:S(2)}) copy-start(f32[2048]{0:T(1024)} %param.25) | copy-start | bytes 24580
  1717.9 23.5 %copy-start.31 = (f32[32]{0:T(128)}, f32[32]{0:T(128)S(1)}, u32[]{:S(2)}) copy-start(f32[32]{0:T(128)S(1)} %pmax.7) | copy-start | bytes 388
  1918.5 10.4 slice-start.2
  (37 other events, 95.4 us)
Sparse Core Ops, SparseCore 0:
  14.4 498.2 all-gather.6
  514.8 357.0 all-gather.12
  874.1 46.3 all-gather.8
  922.5 46.0 all-gather.10
  970.1 45.3 all-gather.14
  1412.9 165.9 all-reduce.4
  1651.8 266.7 all-reduce.6
